TPU v7x, 32 devices: a whole 2x2x4 slice. The times are simulated.
32 devices in a mesh: batch: 4 (over z), pb: 2 (over x), ka: 4 (over y, core).
Axes of the slice: x: 2, y: 2, z: 4, core: 2. Of those that a mesh axis runs over, the one named last changes fastest.
Arguments:
- inputs: bfloat16 [16, 1024, 768], P('batch', ('pb', 'ka')), may hold values from -6 to 6
- block_place: int32 [16, 8], P('batch'), may hold values from 0 to 7, each once within a row
- ln1_gain: float32 [768], replicated, may hold values from 0.1 to 1.9
- ln1_shift: float32 [768], replicated, may hold values from -3 to 3
- w_qkv: bfloat16 [768, 2304], replicated, may hold values from -0.21875 to 0.21875
- w_out: bfloat16 [768, 768], replicated, may hold values from -1.25 to 1.25
- ln2_gain: float32 [768], replicated, may hold values from 0.1 to 1.9
- ln2_shift: float32 [768], replicated, may hold values from -3 to 3
- w_up: bfloat16 [768, 3072], replicated, may hold values from -0.21875 to 0.21875
- w_down: bfloat16 [3072, 768], replicated, may hold values from -0.109375 to 0.109375
- cotangent: bfloat16 [16, 1024, 768], P('batch', ('pb', 'ka')), may hold values from -6 to 6
Outputs:
- outputs: bfloat16 [16, 1024, 768], P('batch', ('pb', 'ka'))
- grad_inputs: bfloat16 [16, 1024, 768], P('batch', ('pb', 'ka'))
- grad_qkv: float32 [768, 2304], P('batch', ('pb', 'ka'))
- grad_proj: float32 [768, 768], P('batch', ('pb', 'ka'))
- grad_up: float32 [768, 3072], P('batch', ('pb', 'ka'))
- grad_down: float32 [3072, 768], P('batch', ('pb', 'ka'))
- grad_norms: float32 [4, 768], P(None, ('pb', 'ka'))
Inputs may be any that keep to these rules, and one draw needn't show every extreme that they name: Each row of block_place lists every number 0 to 7 exactly once.
All inputs are finite; a program needn't handle non-finite values.
Results may differ from a plain program's by a relative error of at most 0.015.
The roundings to bfloat16 on the way count: a program that leaves them out, or rounds other values in their place, can miss the bound.
Values may be sent and summed in bfloat16 or wider, within the bound.
No kernel may reach another device: no remote copies, remote signals or barrier semaphores. Data moves between devices by JAX's collectives and lax.ppermute only.
A program may use at most 192 MiB of HBM per device.

v0:
```python
import jax
import jax.numpy as jnp
from jax import lax
from jax.sharding import PartitionSpec as P

HEADS = 12
HEAD = 64
norm_eps = 1e-05


def merged(part, axis, combine):
    gathered = jax.tree.map(lambda a: lax.all_gather(a, axis), part)

    def take(source):
        return jax.tree.map(lambda a: lax.dynamic_index_in_dim(a, source, 0, False), gathered)

    return lax.fori_loop(
        1, lax.axis_size(axis), lambda source, state: combine(state, take(source)), take(0)
    )


def norm_rows(values, gain_vec, shift_vec):
    average = jnp.mean(values, axis=-1, keepdims=True)
    centred = values - average
    spread = jnp.mean(centred * centred, axis=-1, keepdims=True)
    return centred * lax.rsqrt(spread + norm_eps) * gain_vec + shift_vec


def gelu_tanh(values):
    return jax.nn.gelu(values, approximate=True)


def split_heads(matrix):
    return matrix.reshape(matrix.shape[0], matrix.shape[1], HEADS, HEAD)


def combine_stats(former, latter):
    largest = jnp.maximum(former[0], latter[0])
    return (
        largest,
        former[1] * jnp.exp(former[0] - largest) + latter[1] * jnp.exp(latter[0] - largest),
    )


def tile_scores(query_heads, key_heads):
    return HEAD ** (-0.5) * jnp.einsum(
        "bqhe,bkhe->bhqk", query_heads, key_heads, preferred_element_type=jnp.float32
    )


def tile_weights(scores, visible, row_peak, row_total):
    sign_part = jnp.sign(scores)
    prob_part = (
        jnp.exp(jnp.where(visible, jnp.abs(scores) - row_peak[..., None], -1e30))
        / row_total[..., None]
    )
    return (sign_part, prob_part, sign_part * prob_part)


def shards(
    inputs,
    block_place,
    ln1_gain,
    ln1_shift,
    w_qkv,
    w_out,
    ln2_gain,
    ln2_shift,
    w_up,
    w_down,
    cotangent,
):
    seq_count, block_rows, model_width = inputs.shape
    key_devices = lax.axis_size("ka")
    query_devices = lax.axis_size("pb")
    query_index = lax.axis_index("pb")
    key_index = lax.axis_index("ka")
    offsets = jnp.arange(block_rows, dtype=jnp.int32)
    query_slots = query_index * key_devices + jnp.arange(key_devices, dtype=jnp.int32)
    key_slots = key_index + key_devices * jnp.arange(query_devices, dtype=jnp.int32)
    query_pos = (
        jnp.take(block_place, query_slots, axis=1)[:, :, None] * block_rows + offsets[None, None, :]
    ).reshape(seq_count, key_devices * block_rows)
    key_pos = (
        jnp.take(block_place, key_slots, axis=1)[:, :, None] * block_rows + offsets[None, None, :]
    ).reshape(seq_count, query_devices * block_rows)
    visible = key_pos[:, None, None, :] <= query_pos[:, None, :, None]
    source = inputs.astype(jnp.float32)
    normed1, first_back = jax.vjp(norm_rows, source, ln1_gain, ln1_shift)
    normed1 = normed1.astype(jnp.bfloat16)
    packed = jnp.einsum("btd,de->bte", normed1, w_qkv, preferred_element_type=jnp.float32).astype(
        jnp.bfloat16
    )
    query_half = lax.all_gather(packed[..., :model_width], "ka", axis=1, tiled=True)
    key_set, value_set = (
        lax.all_gather(packed[..., model_width : 2 * model_width], "pb", axis=1, tiled=True),
        lax.all_gather(packed[..., 2 * model_width :], "pb", axis=1, tiled=True),
    )
    query_heads = split_heads(query_half)
    key_heads = split_heads(key_set)
    value_heads = split_heads(value_set)
    scores = tile_scores(query_heads, key_heads)
    magnitude = jnp.abs(scores)
    local_peak = jnp.max(jnp.where(visible, magnitude, -1e30), axis=-1)
    local_sum = jnp.sum(
        jnp.exp(jnp.where(visible, magnitude - local_peak[..., None], -1e30)), axis=-1
    )
    row_peak, row_total = merged((local_peak, local_sum), "ka", combine_stats)
    sign_part, prob_part, signed = tile_weights(scores, visible, row_peak, row_total)
    weights_low = signed.astype(jnp.bfloat16)
    partial_value = jnp.einsum(
        "bhqk,bkhe->bqhe", weights_low, value_heads, preferred_element_type=jnp.float32
    )
    partial_value = partial_value.reshape(seq_count, key_devices * block_rows, model_width)
    attended = lax.psum_scatter(partial_value, "ka", scatter_dimension=1, tiled=True).astype(
        jnp.bfloat16
    )
    residual = source + jnp.einsum(
        "btd,de->bte", attended, w_out, preferred_element_type=jnp.float32
    )
    normed2, second_back = jax.vjp(norm_rows, residual, ln2_gain, ln2_shift)
    normed2 = normed2.astype(jnp.bfloat16)
    pre_act = jnp.einsum("btd,df->btf", normed2, w_up, preferred_element_type=jnp.float32)
    active, gelu_back = jax.vjp(gelu_tanh, pre_act)
    active = active.astype(jnp.bfloat16)
    outputs = (
        residual + jnp.einsum("btf,fd->btd", active, w_down, preferred_element_type=jnp.float32)
    ).astype(jnp.bfloat16)
    grad_down = jnp.einsum("btf,btd->fd", active, cotangent, preferred_element_type=jnp.float32)
    grad_act = jnp.einsum("btd,fd->btf", cotangent, w_down, preferred_element_type=jnp.float32)
    grad_pre = gelu_back(grad_act)[0].astype(jnp.bfloat16)
    grad_up = jnp.einsum("btd,btf->df", normed2, grad_pre, preferred_element_type=jnp.float32)
    grad_normed2 = jnp.einsum("btf,df->btd", grad_pre, w_up, preferred_element_type=jnp.float32)
    grad_res, grad_gain2, grad_shift2 = second_back(grad_normed2)
    grad_res = grad_res + cotangent.astype(jnp.float32)
    grad_z = grad_res.astype(jnp.bfloat16)
    grad_proj = jnp.einsum("btd,bte->de", attended, grad_z, preferred_element_type=jnp.float32)
    grad_att = jnp.einsum("bte,de->btd", grad_z, w_out, preferred_element_type=jnp.float32).astype(
        jnp.bfloat16
    )
    grad_half = lax.all_gather(grad_att, "ka", axis=1, tiled=True)
    grad_heads = split_heads(grad_half)
    scores = tile_scores(query_heads, key_heads)
    sign_part, prob_part, signed = tile_weights(scores, visible, row_peak, row_total)
    weights_low = signed.astype(jnp.bfloat16)
    grad_weights = jnp.einsum(
        "bqhe,bkhe->bhqk", grad_heads, value_heads, preferred_element_type=jnp.float32
    )
    delta_rows = lax.psum(jnp.sum(signed * grad_weights, axis=-1), "ka")
    grad_scores = (
        sign_part * prob_part * (sign_part * grad_weights - delta_rows[..., None])
    ).astype(jnp.bfloat16)
    factor = HEAD ** (-0.5)
    grad_q = factor * jnp.einsum(
        "bhqk,bkhe->bqhe", grad_scores, key_heads, preferred_element_type=jnp.float32
    )
    grad_k = factor * jnp.einsum(
        "bhqk,bqhe->bkhe", grad_scores, query_heads, preferred_element_type=jnp.float32
    )
    grad_v = jnp.einsum(
        "bhqk,bqhe->bkhe", weights_low, grad_heads, preferred_element_type=jnp.float32
    )
    query_grad = lax.psum_scatter(
        grad_q.reshape(seq_count, key_devices * block_rows, model_width).astype(jnp.bfloat16),
        "ka",
        scatter_dimension=1,
        tiled=True,
    ).astype(jnp.float32)
    key_grad, value_grad = (
        lax.psum_scatter(
            grad_k.reshape(seq_count, query_devices * block_rows, model_width).astype(jnp.bfloat16),
            "pb",
            scatter_dimension=1,
            tiled=True,
        ).astype(jnp.float32),
        lax.psum_scatter(
            grad_v.reshape(seq_count, query_devices * block_rows, model_width).astype(jnp.bfloat16),
            "pb",
            scatter_dimension=1,
            tiled=True,
        ).astype(jnp.float32),
    )
    grad_packed = jnp.concatenate([query_grad, key_grad, value_grad], axis=-1).astype(jnp.bfloat16)
    grad_qkv = jnp.einsum("btd,bte->de", normed1, grad_packed, preferred_element_type=jnp.float32)
    grad_normed1 = jnp.einsum("bte,de->btd", grad_packed, w_qkv, preferred_element_type=jnp.float32)
    grad_source, grad_gain1, grad_shift1 = first_back(grad_normed1)
    grad_inputs = (grad_res + grad_source).astype(jnp.bfloat16)
    norm_local = jnp.stack([grad_gain1, grad_shift1, grad_gain2, grad_shift2])
    widened = (
        lax.psum_scatter(
            grad_qkv.astype(jnp.bfloat16), "batch", scatter_dimension=0, tiled=True
        ).astype(jnp.float32),
        lax.psum_scatter(
            grad_proj.astype(jnp.bfloat16), "batch", scatter_dimension=0, tiled=True
        ).astype(jnp.float32),
        lax.psum_scatter(
            grad_up.astype(jnp.bfloat16), "batch", scatter_dimension=0, tiled=True
        ).astype(jnp.float32),
        lax.psum_scatter(
            grad_down.astype(jnp.bfloat16), "batch", scatter_dimension=0, tiled=True
        ).astype(jnp.float32),
    )
    summed = (
        lax.psum_scatter(
            widened[0].astype(jnp.bfloat16), ("pb", "ka"), scatter_dimension=1, tiled=True
        ).astype(jnp.float32),
        lax.psum_scatter(
            widened[1].astype(jnp.bfloat16), ("pb", "ka"), scatter_dimension=1, tiled=True
        ).astype(jnp.float32),
        lax.psum_scatter(
            widened[2].astype(jnp.bfloat16), ("pb", "ka"), scatter_dimension=1, tiled=True
        ).astype(jnp.float32),
        lax.psum_scatter(
            widened[3].astype(jnp.bfloat16), ("pb", "ka"), scatter_dimension=1, tiled=True
        ).astype(jnp.float32),
        lax.psum_scatter(
            norm_local.astype(jnp.bfloat16), ("pb", "ka"), scatter_dimension=1, tiled=True
        ).astype(jnp.float32),
    )
    norm_sum = lax.psum(summed[4], "batch")
    return (outputs, grad_inputs, summed[0], summed[1], summed[2], summed[3], norm_sum)


def solution(mesh):
    placed = (
        P("batch", ("pb", "ka"), None),
        P("batch", None),
        P(),
        P(),
        P(),
        P(),
        P(),
        P(),
        P(),
        P(),
        P("batch", ("pb", "ka"), None),
    )
    return jax.shard_map(
        shards,
        mesh=mesh,
        in_specs=placed,
        out_specs=(
            P("batch", ("pb", "ka"), None),
            P("batch", ("pb", "ka"), None),
            P("batch", ("pb", "ka")),
            P("batch", ("pb", "ka")),
            P("batch", ("pb", "ka")),
            P("batch", ("pb", "ka")),
            P(None, ("pb", "ka")),
        ),
        check_vma=False,
    )
```

profile of v0, /device:TPU:0, one launch (start us, length us, event | category | flops | bytes accessed | tf_op | source)
XLA Modules:
  0.0 959.3 jit_solution(2006295980375979858)
XLA Ops:
  10.8 3.3 convolution_convert_fusion
  20.1 25.6 %all-gather.11.cloned.1.call-done = bf16[4,256,768]{2,1,0:T(8,128)(2,1)} async-done(((bf16[4,128,768]{2,1,0:T(8,128)(2,1)}), bf16[4,256,768]{2,1,0:T(8,128)(2,1)}) %all-gather.11.cloned.1.call-update) | async-done | bytes 1572880 | tf_op jit(solution)/shard_map/all_gather | solution.py:96
  45.7 2.6 copy.64
  48.3 26.2 %all-gather.7.cloned.1.call-done = bf16[4,256,768]{2,1,0:T(8,128)(2,1)} async-done(((bf16[4,128,768]{2,1,0:T(8,128)(2,1)}), bf16[4,256,768]{2,1,0:T(8,128)(2,1)}) %all-gather.7.cloned.1.call-update) | async-done | bytes 1572880 | tf_op jit(solution)/shard_map/all_gather | solution.py:97
  74.5 2.6 copy.62
  77.0 28.1 %all-gather.9.cloned.1.call-done = bf16[4,512,768]{2,1,0:T(8,128)(2,1)} async-done(((bf16[4,128,768]{2,1,0:T(8,128)(2,1)}), bf16[4,512,768]{2,1,0:T(8,128)(2,1)}) %all-gather.9.cloned.1.call-update) | async-done | bytes 3145744 | tf_op jit(solution)/shard_map/all_gather | solution.py:94
  105.2 4.7 copy.63
  109.9 13.1 %select_reduce_fusion = (f32[4,12,512]{2,1,0:T(8,128)S(1)}, f32[4,12,512,256]{2,3,1,0:T(8,128)}) fusion(pred[4,512,256]{1,2,0:T(8,128)(4,1)} %broadcast_compare_fusion, bf16[4,512,12,64]{1,3,2,0:T(8,128)(2,1)} %bitcast.118, bf16[4,256,12,64]{1,3,2,0:T(8,128)(2,1)} %bitcast.123), kind=kOutput, calls=%fused_computation.11 | convolution fusion | flops 830447616 | bytes 30507008 | tf_op jit(solution)/shard_map/bqhe,bkhe->bhqk/dot_general | solution.py:46
  123.0 7.2 all-gather
  130.1 11.7 %exponential_reduce_fusion = f32[4,12,512]{2,1,0:T(8,128)S(1)} fusion(f32[4,12,512,256]{2,3,1,0:T(8,128)} %get-tuple-element.187, f32[4,12,512]{2,1,0:T(8,128)S(1)} %get-tuple-element.186, pred[4,512,256]{1,2,0:T(8,128)(4,1)S(1)} %copy-done.7), kind=kLoop, calls=%fused_computation.10 | loop fusion | flops 31432704 | bytes 25886720 | tf_op jit(solution)/shard_map/reduce_sum | solution.py:105
  142.5 7.5 all-gather.1
  150.8 5.5 while.17
  150.8 1.8 fusion.76
  152.6 1.8 fusion.76
  154.4 1.8 fusion.76
  156.3 21.3 %fusion.11 = f32[4,12,64,512]{3,2,1,0:T(8,128)} fusion(bf16[4,256,12,64]{1,3,2,0:T(8,128)(2,1)} %bitcast.132, f32[4,12,512,256]{2,3,1,0:T(8,128)} %get-tuple-element.187, f32[4,12,512]{2,1,0:T(8,128)} %get-tuple-element.141, f32[4,12,512]{2,1,0:T(8,128)} %get-tuple-element.140, pred[4,512,256]{1,2,0:T(8,128)(4,1)} %broadcast_compare_fusion), kind=kOutput, calls=%fused_computation.28 | convolution fusion | flops 855638016 | bytes 33751040 | tf_op jit(solution)/shard_map/bhqk,bkhe->bqhe/dot_general | solution.py:111
  178.0 57.7 %reduce-scatter.24.cloned.1.call-done = f32[4,128,768]{1,2,0:T(8,128)} async-done(((f32[4,512,768]{1,2,0:T(8,128)}), f32[4,128,768]{1,2,0:T(8,128)}) %reduce-scatter.24.cloned.1.call-update) | async-done | bytes 1572880 | tf_op jit(solution)/shard_map/reduce_scatter | solution.py:115
  235.7 3.0 fusion.56
  239.1 4.9 fusion.19
  244.1 6.2 fusion.8
  250.3 3.5 multiply_reduce_fusion.1
  256.9 1.7 convolution_convert_fusion.1
  259.1 28.1 %all-gather.13.cloned.1.call-done = bf16[4,512,768]{2,1,0:T(8,128)(2,1)} async-done(((bf16[4,128,768]{2,1,0:T(8,128)(2,1)}), bf16[4,512,768]{2,1,0:T(8,128)(2,1)}) %all-gather.13.cloned.1.call-update) | async-done | bytes 3145744 | tf_op jit(solution)/shard_map/all_gather | solution.py:141
  287.3 4.7 copy.71
  291.9 27.0 %multiply_reduce_fusion = (f32[4,12,512]{2,1,0:T(8,128)}, f32[4,12,512,256]{2,3,1,0:T(8,128)}) fusion(f32[4,12,512]{2,1,0:T(8,128)} %get-tuple-element.141, f32[4,12,512]{2,1,0:T(8,128)} %get-tuple-element.140, pred[4,512,256]{1,2,0:T(8,128)(4,1)} %broadcast_compare_fusion, f32[4,12,512,256]{2,3,1,0:T(8,128)} %get-tuple-element.187, ...), kind=kOutput, calls=%fused_computation.8 | convolution fusion | flops 861904896 | bytes 55869440 | tf_op jit(solution)/shard_map/bqhe,bkhe->bhqk/dot_general | solution.py:146
  319.2 31.7 %all-reduce.2.cloned.1.call-done = f32[4,12,512]{2,1,0:T(8,128)} async-done(((f32[4,12,512]{2,1,0:T(8,128)}), f32[4,12,512]{2,1,0:T(8,128)}) %all-reduce.2.cloned.1.call-update) | async-done | bytes 98320 | tf_op jit(solution)/shard_map/psum | solution.py:149
  350.9 21.8 %multiply_convert_fusion = bf16[4,12,512,256]{2,3,1,0:T(8,128)(2,1)S(1)} fusion(f32[4,12,512,256]{2,3,1,0:T(8,128)} %get-tuple-element.192, f32[4,12,512,256]{2,3,1,0:T(8,128)} %get-tuple-element.187, f32[4,12,512]{2,1,0:T(8,128)} %all-reduce.2.cloned.1.call-done, f32[4,12,512]{2,1,0:T(8,128)} %get-tuple-element.141, f32[4,12,512]{2,1,0:T(8,128)} %get-tuple-element.140, ...), kind=kLoop, calls=%fused_computation.7 | loop fusion | flops 69206016 | bytes 63733760 | tf_op jit(solution)/shard_map/convert_element_type | solution.py:152
  372.7 4.5 multiply_convert_fusion.1
  378.3 4.7 copy.73
  383.0 10.7 %multiply_convert_fusion.3 = bf16[4,12,64,256]{3,2,1,0:T(8,128)(2,1)} fusion(bf16[4,512,12,64]{1,3,2,0:T(8,128)(2,1)} %bitcast.119, bf16[4,12,512,256]{2,3,1,0:T(8,128)(2,1)} %copy-done.1), kind=kOutput, calls=%fused_computation.42 | convolution fusion | flops 806879232 | bytes 17301504 | tf_op jit(solution)/shard_map/bhqk,bqhe->bkhe/dot_general | solution.py:157
  393.7 2.6 copy.75
  396.5 22.1 %fusion.32 = bf16[4,12,64,256]{3,2,1,0:T(8,128)(2,1)} fusion(bf16[4,512,12,64]{1,3,2,0:T(8,128)(2,1)} %bitcast.131, f32[4,12,512,256]{2,3,1,0:T(8,128)} %get-tuple-element.187, f32[4,12,512]{2,1,0:T(8,128)} %get-tuple-element.141, f32[4,12,512]{2,1,0:T(8,128)} %get-tuple-element.140, pred[4,512,256]{1,2,0:T(8,128)(4,1)} %broadcast_compare_fusion), kind=kOutput, calls=%fused_computation.55 | convolution fusion | flops 856424448 | bytes 30605312 | tf_op jit(solution)/shard_map/bhqk,bqhe->bkhe/dot_general | solution.py:160
  418.7 2.6 copy.77
  421.3 3.4 bitcast_convert_fusion.3
  424.8 8.4 bitcast_convert_fusion
  434.0 7.4 bitcast_convert_fusion.1
  441.5 2.2 constant_dynamic-update-slice_fusion.2
  443.7 5.6 reduce-scatter.28.cloned.1.call-done
  449.3 2.1 constant_dynamic-update-slice_fusion.1
  451.4 26.3 %reduce-scatter.30.cloned.1.call-done = bf16[4,128,768]{2,1,0:T(8,128)(2,1)} async-done(((bf16[4,256,768]{2,1,0:T(8,128)(2,1)}), bf16[4,128,768]{2,1,0:T(8,128)(2,1)}) %reduce-scatter.30.cloned.1.call-update) | async-done | bytes 786448 | tf_op jit(solution)/shard_map/reduce_scatter | solution.py:176
  477.7 2.1 constant_dynamic-update-slice_fusion
  479.8 6.0 bitcast_convert_fusion.2
  487.8 21.5 %reduce-scatter.34.cloned.1.call-done = bf16[192,768]{1,0:T(8,128)(2,1)} async-done(((bf16[768,768]{1,0:T(8,128)(2,1)}), bf16[192,768]{1,0:T(8,128)(2,1)}) %reduce-scatter.34.cloned.1.call-update) | async-done | bytes 294928 | tf_op jit(solution)/shard_map/reduce_scatter | solution.py:193
  509.3 1.9 copy.92
  511.3 4.0 fusion.39
  517.7 77.7 %reduce-scatter.38.cloned.1.call-done = bf16[768,768]{1,0:T(8,128)(2,1)} async-done(((bf16[3072,768]{1,0:T(8,128)(2,1)}), bf16[768,768]{1,0:T(8,128)(2,1)}) %reduce-scatter.38.cloned.1.call-update) | async-done | bytes 1179664 | tf_op jit(solution)/shard_map/reduce_scatter | solution.py:199
  595.5 2.4 copy.96
  597.9 85.5 %reduce-scatter.36.cloned.1.call-done = bf16[192,3072]{1,0:T(8,128)(2,1)} async-done(((bf16[768,3072]{1,0:T(8,128)(2,1)}), bf16[192,3072]{1,0:T(8,128)(2,1)}) %reduce-scatter.36.cloned.1.call-update) | async-done | bytes 1179664 | tf_op jit(solution)/shard_map/reduce_scatter | solution.py:196
  683.5 2.5 copy.94
  686.4 66.5 %reduce-scatter.32.cloned.1.call-done = bf16[192,2304]{1,0:T(8,128)(2,1)} async-done(((bf16[768,2304]{1,0:T(8,128)(2,1)}), bf16[192,2304]{1,0:T(8,128)(2,1)}) %reduce-scatter.32.cloned.1.call-update) | async-done | bytes 884752 | tf_op jit(solution)/shard_map/reduce_scatter | solution.py:190
  752.9 2.3 copy.90
  755.2 9.3 add_convert_fusion.1
  764.5 25.9 %reduce-scatter.42.cloned.1.call-done = bf16[96,192]{1,0:T(8,128)(2,1)} async-done(((bf16[768,192]{1,0:T(8,128)(2,1)}), bf16[96,192]{1,0:T(8,128)(2,1)}) %reduce-scatter.42.cloned.1.call-update) | async-done | bytes 36880
  794.1 3.9 add_convert_fusion
  798.0 29.6 %reduce-scatter.48.cloned.1.call-done = bf16[96,4]{1,0:T(8,128)(2,1)} async-done(((bf16[768,4]{1,0:T(8,128)(2,1)}), bf16[96,4]{1,0:T(8,128)(2,1)}) %reduce-scatter.48.cloned.1.call-update) | async-done | bytes 784
  828.4 12.2 %psum.15 = f32[4,96]{1,0:T(4,128)} all-reduce(bf16[4,96]{1,0:T(4,128)(2,1)S(1)} %copy.99), channel_id=1, replica_groups=mesh['batch'=4,'pb'=2,'ka'=4] {'batch'}, use_global_device_ids=true, to_apply=%region_31.32 | all-reduce | flops 384 | bytes 2304 | tf_op jit(solution)/shard_map/psum | solution.py:220
  840.6 26.7 %reduce-scatter.46.cloned.1.call-done = bf16[96,768]{1,0:T(8,128)(2,1)} async-done(((bf16[768,768]{1,0:T(8,128)(2,1)}), bf16[96,768]{1,0:T(8,128)(2,1)}) %reduce-scatter.46.cloned.1.call-update) | async-done | bytes 147472
  867.4 1.7 copy.97
  869.1 1.8 copy.81
  870.9 38.0 %reduce-scatter.44.cloned.1.call-done = bf16[384,192]{1,0:T(8,128)(2,1)} async-done(((bf16[3072,192]{1,0:T(8,128)(2,1)}), bf16[384,192]{1,0:T(8,128)(2,1)}) %reduce-scatter.44.cloned.1.call-update) | async-done | bytes 147472
  908.8 1.7 copy.95
  910.6 1.6 convert_element_type.138
  912.2 36.4 %reduce-scatter.40.cloned.1.call-done = bf16[288,192]{1,0:T(8,128)(2,1)} async-done(((bf16[2304,192]{1,0:T(8,128)(2,1)}), bf16[288,192]{1,0:T(8,128)(2,1)}) %reduce-scatter.40.cloned.1.call-update) | async-done | bytes 110608
  948.6 1.7 copy.91
  (171 shorter events, 28.5 us)
Async XLA Ops:
  7.2 3.6 copy-start
  7.2 38.5 %all-gather.11.cloned.1.call-start = ((), (), s32[]{:S(2)}) async-start(), calls=%async_computation.15 | async-start | bytes 2359296 | tf_op jit(solution)/shard_map/all_gather | solution.py:96
  8.7 5.4 copy-start.13
  10.2 0.6 copy-start.20
  10.8 3.3 copy-start.15
  14.1 3.1 copy-start.32
  15.6 58.8 %all-gather.7.cloned.1.call-start = ((), (), s32[]{:S(2)}) async-start(), calls=%async_computation.13 | async-start | bytes 2359296 | tf_op jit(solution)/shard_map/all_gather | solution.py:97
  16.4 88.8 %all-gather.9.cloned.1.call-start = ((), (), s32[]{:S(2)}) async-start(), calls=%async_computation.14 | async-start | bytes 3932160 | tf_op jit(solution)/shard_map/all_gather | solution.py:94
  17.1 218.6 %reduce-scatter.24.cloned.1.call-start = ((), (), s32[]{:S(2)}) async-start(), calls=%async_computation.16 | async-start | bytes 7864320 | tf_op jit(solution)/shard_map/reduce_scatter | solution.py:115
  109.9 20.3 %copy-start.7 = (pred[4,512,256]{1,2,0:T(8,128)(4,1)S(1)}, pred[4,512,256]{1,2,0:T(8,128)(4,1)}, u32[]{:S(2)}) copy-start(pred[4,512,256]{1,2,0:T(8,128)(4,1)} %broadcast_compare_fusion) | copy-start | bytes 1572868
  130.1 11.7 %copy-start.8 = (f32[16,12,512]{2,1,0:T(8,128)}, f32[16,12,512]{2,1,0:T(8,128)S(1)}, u32[]{:S(2)}) copy-start(f32[16,12,512]{2,1,0:T(8,128)S(1)} %all-gather) | copy-start | bytes 1179652
  149.9 0.8 copy-start.9
  177.6 61.4 %copy-start.30 = (f32[768]{0:T(1024)S(1)}, f32[768]{0:T(1024)}, u32[]{:S(2)}) copy-start(f32[768]{0:T(1024)} %param.19) | copy-start | bytes 9220
  177.7 61.4 %copy-start.34 = (f32[768]{0:T(1024)S(1)}, f32[768]{0:T(1024)}, u32[]{:S(2)}) copy-start(f32[768]{0:T(1024)} %param.20) | copy-start | bytes 9220
  177.7 109.6 %all-gather.13.cloned.1.call-start = ((), (), s32[]{:S(2)}) async-start(), calls=%async_computation.17 | async-start | bytes 3932160 | tf_op jit(solution)/shard_map/all_gather | solution.py:141
  235.7 8.4 slice-start.2
  238.7 15.2 %copy-start.3 = (f32[4,128,768]{2,1,0:T(8,128)}, f32[4,128,768]{2,1,0:T(8,128)S(1)}, u32[]{:S(2)}) copy-start(f32[4,128,768]{2,1,0:T(8,128)S(1)} %get-tuple-element.189) | copy-start | bytes 4718596
  238.7 15.2 %copy-start.18 = (f32[4,128]{1,0:T(4,128)}, f32[4,128]{1,0:T(4,128)S(1)}, u32[]{:S(2)}) copy-start(f32[4,128]{1,0:T(4,128)S(1)} %broadcast_multiply_fusion) | copy-start | bytes 6148
  239.1 14.8 %copy-start.28 = (f32[4,128]{1,0:T(4,128)}, f32[4,128]{1,0:T(4,128)S(1)}, u32[]{:S(2)}) copy-start(f32[4,128]{1,0:T(4,128)S(1)} %fusion.51) | copy-start | bytes 6148
  239.1 5.0 copy-start.11
  239.1 5.0 slice-start.3
  239.1 11.2 %slice-start = ((s8[4718592]{0:T(1024)(128)(4,1)}), s8[4194304]{0:T(1024)(128)(4,1)S(1)}, s32[]{:S(2)}) async-start(s8[4718592]{0:T(1024)(128)(4,1)} %bitcast.142), calls=%async_computation.31 | async-start | bytes 8388608
  244.1 6.2 copy-start.37
  244.1 6.2 slice-start.1
  250.3 3.5 copy-start.38
  253.9 3.0 copy-start.12
  254.5 1.2 copy-start.4
  254.6 1.4 copy-start.22
  256.0 0.9 copy-start.10
  258.6 92.3 %all-reduce.2.cloned.1.call-start = ((), (), s32[]{:S(2)}) async-start(), calls=%async_computation.18 | async-start | bytes 262144 | tf_op jit(solution)/shard_map/psum | solution.py:149
  319.0 122.5 %reduce-scatter.26.cloned.1.call-start = ((), (), s32[]{:S(2)}) async-start(), calls=%async_computation.19 | async-start | bytes 3932160 | tf_op jit(solution)/shard_map/reduce_scatter | solution.py:163
  350.9 21.8 %copy-start.5 = (bf16[4,256,768]{1,2,0:T(8,128)(2,1)S(1)}, bf16[4,256,768]{1,2,0:T(8,128)(2,1)}, u32[]{:S(2)}) copy-start(bf16[4,256,768]{1,2,0:T(8,128)(2,1)} %copy.64) | copy-start | bytes 4718596
  372.7 5.5 copy-start.1
  382.9 66.3 %reduce-scatter.28.cloned.1.call-start = ((), (), s32[]{:S(2)}) async-start(), calls=%async_computation.20 | async-start | bytes 2359296 | tf_op jit(solution)/shard_map/reduce_scatter | solution.py:170
  396.3 81.4 %reduce-scatter.30.cloned.1.call-start = ((), (), s32[]{:S(2)}) async-start(), calls=%async_computation.21 | async-start | bytes 2359296 | tf_op jit(solution)/shard_map/reduce_scatter | solution.py:176
  421.3 88.0 %reduce-scatter.34.cloned.1.call-start = ((), (), s32[]{:S(2)}) async-start(), calls=%async_computation.23 | async-start | bytes 1474560 | tf_op jit(solution)/shard_map/reduce_scatter | solution.py:193
  424.8 170.7 %reduce-scatter.38.cloned.1.call-start = ((), (), s32[]{:S(2)}) async-start(), calls=%async_computation.25 | async-start | bytes 5898240 | tf_op jit(solution)/shard_map/reduce_scatter | solution.py:199
  433.3 0.7 copy-start.19
  433.3 0.7 copy-start.29
  433.3 0.7 copy-start.31
  433.3 0.7 copy-start.35
  433.3 250.2 %reduce-scatter.36.cloned.1.call-start = ((), (), s32[]{:S(2)}) async-start(), calls=%async_computation.24 | async-start | bytes 5898240 | tf_op jit(solution)/shard_map/reduce_scatter | solution.py:196
  441.4 38.4 %copy-start.14 = (f32[4,128]{1,0:T(4,128)S(1)}, f32[4,128]{1,0:T(4,128)}, u32[]{:S(2)}) copy-start(f32[4,128]{1,0:T(4,128)} %copy-done.13) | copy-start | bytes 6148
  441.4 38.4 %copy-start.16 = (f32[4,128]{1,0:T(4,128)S(1)}, f32[4,128]{1,0:T(4,128)}, u32[]{:S(2)}) copy-start(f32[4,128]{1,0:T(4,128)} %copy-done.15) | copy-start | bytes 6148
  441.4 38.4 %copy-start.24 = (f32[768]{0:T(1024)S(1)}, f32[768]{0:T(1024)}, u32[]{:S(2)}) copy-start(f32[768]{0:T(1024)} %param.15) | copy-start | bytes 9220
  441.4 38.4 %copy-start.36 = (f32[768]{0:T(1024)S(1)}, f32[768]{0:T(1024)}, u32[]{:S(2)}) copy-start(f32[768]{0:T(1024)} %param.16) | copy-start | bytes 9220
  441.4 311.5 %reduce-scatter.32.cloned.1.call-start = ((), (), s32[]{:S(2)}) async-start(), calls=%async_computation.22 | async-start | bytes 4423680 | tf_op jit(solution)/shard_map/reduce_scatter | solution.py:190
  485.8 1.3 copy-start.33
  485.9 304.6 %reduce-scatter.42.cloned.1.call-start = ((), (), s32[]{:S(2)}) async-start(), calls=%async_computation.27 | async-start | bytes 442368
  511.2 4.1 copy-start.21
  511.2 316.4 %reduce-scatter.48.cloned.1.call-start = ((), (), s32[]{:S(2)}) async-start(), calls=%async_computation.30 | async-start | bytes 221184
  511.2 4.1 copy-start.2
  511.2 4.1 copy-start.25
  511.3 5.5 copy-start.26
  511.3 5.5 copy-start.27
  515.3 1.5 copy-start.6
  517.7 349.7 %reduce-scatter.46.cloned.1.call-start = ((), (), s32[]{:S(2)}) async-start(), calls=%async_computation.29 | async-start | bytes 1327104
  597.9 310.9 %reduce-scatter.44.cloned.1.call-start = ((), (), s32[]{:S(2)}) async-start(), calls=%async_computation.28 | async-start | bytes 1769472
  686.0 262.6 %reduce-scatter.40.cloned.1.call-start = ((), (), s32[]{:S(2)}) async-start(), calls=%async_computation.26 | async-start | bytes 1327104
  755.2 38.9 %copy-start.17 = (f32[4,128]{1,0:T(4,128)S(1)}, f32[4,128]{1,0:T(4,128)}, u32[]{:S(2)}) copy-start(f32[4,128]{1,0:T(4,128)} %copy-done.15) | copy-start | bytes 6148
  755.2 38.9 %copy-start.23 = (f32[4,128]{1,0:T(4,128)S(1)}, f32[4,128]{1,0:T(4,128)}, u32[]{:S(2)}) copy-start(f32[4,128]{1,0:T(4,128)} %copy-done.22) | copy-start | bytes 6148
Sparse Core Ops, SparseCore 0:
  15.8 29.8 all-gather.10
  47.2 27.1 all-gather.6
  76.6 28.5 all-gather.8
  177.8 57.8 reduce-scatter.23
  258.7 28.4 all-gather.12
  319.1 31.7 all-reduce.1
  383.1 37.7 reduce-scatter.25
  423.1 26.1 reduce-scatter.27
  451.5 26.1 reduce-scatter.29
  479.9 29.3 reduce-scatter.33
  511.6 83.8 reduce-scatter.37
  597.6 85.7 reduce-scatter.35
  685.8 67.0 reduce-scatter.31
  756.4 34.0 reduce-scatter.41
  793.9 33.6 reduce-scatter.47
  830.6 36.6 reduce-scatter.45
  870.5 38.2 reduce-scatter.43
  911.9 36.6 reduce-scatter.39
where the time goes:
time: 967 us; the launch traced here: 959 us
  waiting for transfers between devices  639 us (66%)
  matrix products  160 us (17%)
  local copies, waits for them, and re-layouts  60.4 us (6%)
  other arithmetic  55.3 us (6%)
  blocking collectives  26.9 us (3%)
  between operations  15.4 us (2%)
    unnamed x23, waiting for transfers between devices  158 us
    reduce_scatter x1, waiting for transfers between devices, shards(): lax.psum_scatter(grad_up.astype(jnp.bfloat16), 'batch', scatter_dimension...  85.5 us
    reduce_scatter x1, waiting for transfers between devices, shards(): lax.psum_scatter(grad_down.astype(jnp.bfloat16), 'batch', scatter_dimensi...  77.7 us
    reduce_scatter x1, waiting for transfers between devices, shards(): lax.psum_scatter(grad_qkv.astype(jnp.bfloat16), 'batch', scatter_dimensio...  66.5 us
    reduce_scatter x1, waiting for transfers between devices, shards(): lax.psum_scatter(partial_value, 'ka', scatter_dimension=1, tiled=True)  57.7 us
    psum x1, waiting for transfers between devices, shards(): delta_rows = lax.psum(jnp.sum(signed * grad_weights, axis=-1), 'ka')  31.7 us
    all_gather x1, waiting for transfers between devices, shards(): grad_half = lax.all_gather(grad_att, 'ka', axis=1, tiled=True)  28.1 us
    all_gather x1, waiting for transfers between devices, shards(): lax.all_gather(packed[..., :model_width], 'ka', axis=1, tiled=True)  28.1 us
  transfers between devices with their start and end apart: 18, of which 17 were waited for; matrix products, arithmetic and copies ran while one was open for 12% of the time, Pallas kernels for 0%

commit v1 on v0

--- a/solution.py
+++ b/solution.py
@@ -146,7 +146,7 @@
     grad_weights = jnp.einsum(
         "bqhe,bkhe->bhqk", grad_heads, value_heads, preferred_element_type=jnp.float32
     )
-    delta_rows = lax.psum(jnp.sum(signed * grad_weights, axis=-1), "ka")
+    delta_rows = jnp.sum(lax.all_gather(jnp.sum(signed * grad_weights, axis=-1), "ka"), axis=0)
     grad_scores = (
         sign_part * prob_part * (sign_part * grad_weights - delta_rows[..., None])
     ).astype(jnp.bfloat16)

time: 967 us -> 946 us (0.978)
  waiting for transfers between devices: 639 us -> 609 us
    psum x1 -> x0, waiting for transfers between devices: 31.7 us -> none  [shards(): delta_rows = lax.psum(jnp.sum(signed * grad_weights, axis=-1), 'ka')]
    unnamed x23 -> x22, waiting for transfers between devices: 158 us -> 159 us
  transfers between devices with their start and end apart: 18 -> 17, of which waited for: 17 -> 16; matrix products, arithmetic and copies ran while one was open for 12% -> 13% of each run, Pallas kernels for 0% -> 0%
where the time goes in v1:
time: 946 us; the launch traced here: 938 us
  waiting for transfers between devices  609 us (64%)
  matrix products  160 us (17%)
  local copies, waits for them, and re-layouts  60.4 us (6%)
  other arithmetic  57 us (6%)
  blocking collectives  34.9 us (4%)
  between operations  15.1 us (2%)
    unnamed x22, waiting for transfers between devices  159 us
    reduce_scatter x1, waiting for transfers between devices, shards(): lax.psum_scatter(grad_up.astype(jnp.bfloat16), 'batch', scatter_dimension...  85.7 us
    reduce_scatter x1, waiting for transfers between devices, shards(): lax.psum_scatter(grad_down.astype(jnp.bfloat16), 'batch', scatter_dimensi...  77.6 us
    reduce_scatter x1, waiting for transfers between devices, shards(): lax.psum_scatter(grad_qkv.astype(jnp.bfloat16), 'batch', scatter_dimensio...  66.4 us
    reduce_scatter x1, waiting for transfers between devices, shards(): lax.psum_scatter(partial_value, 'ka', scatter_dimension=1, tiled=True)  57.7 us
    all_gather x1, waiting for transfers between devices, shards(): grad_half = lax.all_gather(grad_att, 'ka', axis=1, tiled=True)  28.2 us
    all_gather x1, waiting for transfers between devices, shards(): lax.all_gather(packed[..., :model_width], 'ka', axis=1, tiled=True)  28.1 us
    unnamed x102, local copies, waits for them, and re-layouts  27.9 us
  transfers between devices with their start and end apart: 17, of which 16 were waited for; matrix products, arithmetic and copies ran while one was open for 13% of the time, Pallas kernels for 0%

profile of v1, /device:TPU:0, one launch (start us, length us, event | category | flops | bytes accessed | tf_op | source)
XLA Modules:
  0.0 938.1 jit_solution(15462200426140176571)
XLA Ops:
  10.8 3.3 convolution_convert_fusion
  20.1 25.6 %all-gather.12.cloned.1.call-done = bf16[4,256,768]{2,1,0:T(8,128)(2,1)} async-done(((bf16[4,128,768]{2,1,0:T(8,128)(2,1)}), bf16[4,256,768]{2,1,0:T(8,128)(2,1)}) %all-gather.12.cloned.1.call-update) | async-done | bytes 1572880 | tf_op jit(solution)/shard_map/all_gather | solution.py:96
  45.7 2.6 copy.64
  48.3 26.2 %all-gather.8.cloned.1.call-done = bf16[4,256,768]{2,1,0:T(8,128)(2,1)} async-done(((bf16[4,128,768]{2,1,0:T(8,128)(2,1)}), bf16[4,256,768]{2,1,0:T(8,128)(2,1)}) %all-gather.8.cloned.1.call-update) | async-done | bytes 1572880 | tf_op jit(solution)/shard_map/all_gather | solution.py:97
  74.5 2.6 copy.62
  77.1 28.1 %all-gather.10.cloned.1.call-done = bf16[4,512,768]{2,1,0:T(8,128)(2,1)} async-done(((bf16[4,128,768]{2,1,0:T(8,128)(2,1)}), bf16[4,512,768]{2,1,0:T(8,128)(2,1)}) %all-gather.10.cloned.1.call-update) | async-done | bytes 3145744 | tf_op jit(solution)/shard_map/all_gather | solution.py:94
  105.2 4.7 copy.63
  109.8 13.1 %select_reduce_fusion = (f32[4,12,512]{2,1,0:T(8,128)S(1)}, f32[4,12,512,256]{2,3,1,0:T(8,128)}) fusion(pred[4,512,256]{1,2,0:T(8,128)(4,1)} %broadcast_compare_fusion, bf16[4,512,12,64]{1,3,2,0:T(8,128)(2,1)} %bitcast.119, bf16[4,256,12,64]{1,3,2,0:T(8,128)(2,1)} %bitcast.124), kind=kOutput, calls=%fused_computation.11 | convolution fusion | flops 830447616 | bytes 30507008 | tf_op jit(solution)/shard_map/bqhe,bkhe->bhqk/dot_general | solution.py:46
  122.9 7.2 all-gather
  130.1 11.7 %exponential_reduce_fusion = f32[4,12,512]{2,1,0:T(8,128)S(1)} fusion(f32[4,12,512,256]{2,3,1,0:T(8,128)} %get-tuple-element.187, f32[4,12,512]{2,1,0:T(8,128)S(1)} %get-tuple-element.186, pred[4,512,256]{1,2,0:T(8,128)(4,1)S(1)} %copy-done.7), kind=kLoop, calls=%fused_computation.10 | loop fusion | flops 31432704 | bytes 25886720 | tf_op jit(solution)/shard_map/reduce_sum | solution.py:105
  142.4 7.5 all-gather.1
  150.7 5.5 while.17
  150.7 1.8 fusion.76
  152.6 1.8 fusion.76
  154.4 1.8 fusion.76
  156.2 21.3 %fusion.11 = f32[4,12,64,512]{3,2,1,0:T(8,128)} fusion(bf16[4,256,12,64]{1,3,2,0:T(8,128)(2,1)} %bitcast.134, f32[4,12,512,256]{2,3,1,0:T(8,128)} %get-tuple-element.187, f32[4,12,512]{2,1,0:T(8,128)} %get-tuple-element.141, f32[4,12,512]{2,1,0:T(8,128)} %get-tuple-element.140, pred[4,512,256]{1,2,0:T(8,128)(4,1)} %broadcast_compare_fusion), kind=kOutput, calls=%fused_computation.28 | convolution fusion | flops 855638016 | bytes 33751040 | tf_op jit(solution)/shard_map/bhqk,bkhe->bqhe/dot_general | solution.py:111
  177.9 57.7 %reduce-scatter.24.cloned.1.call-done = f32[4,128,768]{1,2,0:T(8,128)} async-done(((f32[4,512,768]{1,2,0:T(8,128)}), f32[4,128,768]{1,2,0:T(8,128)}) %reduce-scatter.24.cloned.1.call-update) | async-done | bytes 1572880 | tf_op jit(solution)/shard_map/reduce_scatter | solution.py:115
  235.6 3.0 fusion.56
  239.1 4.9 fusion.19
  244.1 6.2 fusion.8
  250.3 3.5 multiply_reduce_fusion.1
  256.8 1.7 convolution_convert_fusion.1
  259.1 28.2 %all-gather.14.cloned.1.call-done = bf16[4,512,768]{2,1,0:T(8,128)(2,1)} async-done(((bf16[4,128,768]{2,1,0:T(8,128)(2,1)}), bf16[4,512,768]{2,1,0:T(8,128)(2,1)}) %all-gather.14.cloned.1.call-update) | async-done | bytes 3145744 | tf_op jit(solution)/shard_map/all_gather | solution.py:141
  287.2 4.6 copy.71
  291.9 27.0 %multiply_reduce_fusion = (f32[4,12,512]{2,1,0:T(8,128)}, f32[4,12,512,256]{2,3,1,0:T(8,128)}) fusion(f32[4,12,512]{2,1,0:T(8,128)} %get-tuple-element.141, f32[4,12,512]{2,1,0:T(8,128)} %get-tuple-element.140, pred[4,512,256]{1,2,0:T(8,128)(4,1)} %broadcast_compare_fusion, f32[4,12,512,256]{2,3,1,0:T(8,128)} %get-tuple-element.187, ...), kind=kOutput, calls=%fused_computation.8 | convolution fusion | flops 861904896 | bytes 55869440 | tf_op jit(solution)/shard_map/bqhe,bkhe->bhqk/dot_general | solution.py:146
  318.9 8.1 all-gather.2
  327.0 1.7 reduce_sum.146
  328.7 21.8 %multiply_convert_fusion = bf16[4,12,512,256]{2,3,1,0:T(8,128)(2,1)S(1)} fusion(f32[4,12,512,256]{2,3,1,0:T(8,128)} %get-tuple-element.192, f32[4,12,512,256]{2,3,1,0:T(8,128)} %get-tuple-element.187, f32[4,12,512]{2,1,0:T(8,128)} %reduce_sum.146, f32[4,12,512]{2,1,0:T(8,128)} %get-tuple-element.141, f32[4,12,512]{2,1,0:T(8,128)} %get-tuple-element.140, ...), kind=kLoop, calls=%fused_computation.7 | loop fusion | flops 69206016 | bytes 63733760 | tf_op jit(solution)/shard_map/convert_element_type | solution.py:152
  350.6 4.5 multiply_convert_fusion.1
  356.1 4.6 copy.73
  360.8 10.6 %multiply_convert_fusion.3 = bf16[4,12,64,256]{3,2,1,0:T(8,128)(2,1)} fusion(bf16[4,512,12,64]{1,3,2,0:T(8,128)(2,1)} %bitcast.120, bf16[4,12,512,256]{2,3,1,0:T(8,128)(2,1)} %copy-done.1), kind=kOutput, calls=%fused_computation.42 | convolution fusion | flops 806879232 | bytes 17301504 | tf_op jit(solution)/shard_map/bhqk,bqhe->bkhe/dot_general | solution.py:157
  371.4 2.6 copy.75
  374.3 21.9 %fusion.32 = bf16[4,12,64,256]{3,2,1,0:T(8,128)(2,1)} fusion(bf16[4,512,12,64]{1,3,2,0:T(8,128)(2,1)} %bitcast.132, f32[4,12,512,256]{2,3,1,0:T(8,128)} %get-tuple-element.187, f32[4,12,512]{2,1,0:T(8,128)} %get-tuple-element.141, f32[4,12,512]{2,1,0:T(8,128)} %get-tuple-element.140, pred[4,512,256]{1,2,0:T(8,128)(4,1)} %broadcast_compare_fusion), kind=kOutput, calls=%fused_computation.55 | convolution fusion | flops 856424448 | bytes 30605312 | tf_op jit(solution)/shard_map/bhqk,bqhe->bkhe/dot_general | solution.py:160
  396.2 2.6 copy.77
  398.9 3.5 bitcast_convert_fusion.3
  402.4 8.4 bitcast_convert_fusion
  411.6 7.4 bitcast_convert_fusion.1
  419.1 2.1 constant_dynamic-update-slice_fusion.2
  421.2 7.0 reduce-scatter.28.cloned.1.call-done
  428.2 2.2 constant_dynamic-update-slice_fusion.1
  430.4 26.3 %reduce-scatter.30.cloned.1.call-done = bf16[4,128,768]{2,1,0:T(8,128)(2,1)} async-done(((bf16[4,256,768]{2,1,0:T(8,128)(2,1)}), bf16[4,128,768]{2,1,0:T(8,128)(2,1)}) %reduce-scatter.30.cloned.1.call-update) | async-done | bytes 786448 | tf_op jit(solution)/shard_map/reduce_scatter | solution.py:176
  456.6 2.1 constant_dynamic-update-slice_fusion
  458.8 6.0 bitcast_convert_fusion.2
  466.7 21.6 %reduce-scatter.34.cloned.1.call-done = bf16[192,768]{1,0:T(8,128)(2,1)} async-done(((bf16[768,768]{1,0:T(8,128)(2,1)}), bf16[192,768]{1,0:T(8,128)(2,1)}) %reduce-scatter.34.cloned.1.call-update) | async-done | bytes 294928 | tf_op jit(solution)/shard_map/reduce_scatter | solution.py:193
  488.3 1.9 copy.92
  490.3 4.0 fusion.39
  496.8 77.6 %reduce-scatter.38.cloned.1.call-done = bf16[768,768]{1,0:T(8,128)(2,1)} async-done(((bf16[3072,768]{1,0:T(8,128)(2,1)}), bf16[768,768]{1,0:T(8,128)(2,1)}) %reduce-scatter.38.cloned.1.call-update) | async-done | bytes 1179664 | tf_op jit(solution)/shard_map/reduce_scatter | solution.py:199
  574.4 2.4 copy.96
  576.8 85.7 %reduce-scatter.36.cloned.1.call-done = bf16[192,3072]{1,0:T(8,128)(2,1)} async-done(((bf16[768,3072]{1,0:T(8,128)(2,1)}), bf16[192,3072]{1,0:T(8,128)(2,1)}) %reduce-scatter.36.cloned.1.call-update) | async-done | bytes 1179664 | tf_op jit(solution)/shard_map/reduce_scatter | solution.py:196
  662.5 2.5 copy.94
  665.4 66.4 %reduce-scatter.32.cloned.1.call-done = bf16[192,2304]{1,0:T(8,128)(2,1)} async-done(((bf16[768,2304]{1,0:T(8,128)(2,1)}), bf16[192,2304]{1,0:T(8,128)(2,1)}) %reduce-scatter.32.cloned.1.call-update) | async-done | bytes 884752 | tf_op jit(solution)/shard_map/reduce_scatter | solution.py:190
  731.8 2.3 copy.90
  734.1 9.3 add_convert_fusion.1
  743.4 26.1 %reduce-scatter.42.cloned.1.call-done = bf16[96,192]{1,0:T(8,128)(2,1)} async-done(((bf16[768,192]{1,0:T(8,128)(2,1)}), bf16[96,192]{1,0:T(8,128)(2,1)}) %reduce-scatter.42.cloned.1.call-update) | async-done | bytes 36880
  773.1 3.9 add_convert_fusion
  777.0 29.6 %reduce-scatter.48.cloned.1.call-done = bf16[96,4]{1,0:T(8,128)(2,1)} async-done(((bf16[768,4]{1,0:T(8,128)(2,1)}), bf16[96,4]{1,0:T(8,128)(2,1)}) %reduce-scatter.48.cloned.1.call-update) | async-done | bytes 784
  807.4 12.2 %psum.7 = f32[4,96]{1,0:T(4,128)} all-reduce(bf16[4,96]{1,0:T(4,128)(2,1)S(1)} %copy.99), channel_id=1, replica_groups=mesh['batch'=4,'pb'=2,'ka'=4] {'batch'}, use_global_device_ids=true, to_apply=%region_31.32 | all-reduce | flops 384 | bytes 2304 | tf_op jit(solution)/shard_map/psum | solution.py:220
  819.6 26.8 %reduce-scatter.46.cloned.1.call-done = bf16[96,768]{1,0:T(8,128)(2,1)} async-done(((bf16[768,768]{1,0:T(8,128)(2,1)}), bf16[96,768]{1,0:T(8,128)(2,1)}) %reduce-scatter.46.cloned.1.call-update) | async-done | bytes 147472
  846.4 1.7 copy.97
  848.1 1.8 copy.81
  849.9 38.1 %reduce-scatter.44.cloned.1.call-done = bf16[384,192]{1,0:T(8,128)(2,1)} async-done(((bf16[3072,192]{1,0:T(8,128)(2,1)}), bf16[384,192]{1,0:T(8,128)(2,1)}) %reduce-scatter.44.cloned.1.call-update) | async-done | bytes 147472
  887.9 1.7 copy.95
  891.3 36.4 %reduce-scatter.40.cloned.1.call-done = bf16[288,192]{1,0:T(8,128)(2,1)} async-done(((bf16[2304,192]{1,0:T(8,128)(2,1)}), bf16[288,192]{1,0:T(8,128)(2,1)}) %reduce-scatter.40.cloned.1.call-update) | async-done | bytes 110608
  927.7 1.7 copy.91
  (170 shorter events, 29.9 us)
Async XLA Ops:
  7.2 3.6 copy-start
  7.2 38.5 %all-gather.12.cloned.1.call-start = ((), (), s32[]{:S(2)}) async-start(), calls=%async_computation.15 | async-start | bytes 2359296 | tf_op jit(solution)/shard_map/all_gather | solution.py:96
  8.7 5.4 copy-start.13
  10.2 0.6 copy-start.20
  10.8 3.3 copy-start.15
  14.1 3.1 copy-start.32
  15.6 58.8 %all-gather.8.cloned.1.call-start = ((), (), s32[]{:S(2)}) async-start(), calls=%async_computation.13 | async-start | bytes 2359296 | tf_op jit(solution)/shard_map/all_gather | solution.py:97
  16.4 88.8 %all-gather.10.cloned.1.call-start = ((), (), s32[]{:S(2)}) async-start(), calls=%async_computation.14 | async-start | bytes 3932160 | tf_op jit(solution)/shard_map/all_gather | solution.py:94
  17.1 218.5 %reduce-scatter.24.cloned.1.call-start = ((), (), s32[]{:S(2)}) async-start(), calls=%async_computation.16 | async-start | bytes 7864320 | tf_op jit(solution)/shard_map/reduce_scatter | solution.py:115
  109.8 20.2 %copy-start.7 = (pred[4,512,256]{1,2,0:T(8,128)(4,1)S(1)}, pred[4,512,256]{1,2,0:T(8,128)(4,1)}, u32[]{:S(2)}) copy-start(pred[4,512,256]{1,2,0:T(8,128)(4,1)} %broadcast_compare_fusion) | copy-start | bytes 1572868
  130.1 11.7 %copy-start.8 = (f32[16,12,512]{2,1,0:T(8,128)}, f32[16,12,512]{2,1,0:T(8,128)S(1)}, u32[]{:S(2)}) copy-start(f32[16,12,512]{2,1,0:T(8,128)S(1)} %all-gather) | copy-start | bytes 1179652
  149.9 0.8 copy-start.9
  177.6 61.4 %copy-start.30 = (f32[768]{0:T(1024)S(1)}, f32[768]{0:T(1024)}, u32[]{:S(2)}) copy-start(f32[768]{0:T(1024)} %param.19) | copy-start | bytes 9220
  177.6 61.4 %copy-start.34 = (f32[768]{0:T(1024)S(1)}, f32[768]{0:T(1024)}, u32[]{:S(2)}) copy-start(f32[768]{0:T(1024)} %param.20) | copy-start | bytes 9220
  177.6 109.6 %all-gather.14.cloned.1.call-start = ((), (), s32[]{:S(2)}) async-start(), calls=%async_computation.17 | async-start | bytes 3932160 | tf_op jit(solution)/shard_map/all_gather | solution.py:141
  235.6 8.4 slice-start.2
  238.7 15.2 %copy-start.3 = (f32[4,128,768]{2,1,0:T(8,128)}, f32[4,128,768]{2,1,0:T(8,128)S(1)}, u32[]{:S(2)}) copy-start(f32[4,128,768]{2,1,0:T(8,128)S(1)} %get-tuple-element.189) | copy-start | bytes 4718596
  238.7 15.2 %copy-start.18 = (f32[4,128]{1,0:T(4,128)}, f32[4,128]{1,0:T(4,128)S(1)}, u32[]{:S(2)}) copy-start(f32[4,128]{1,0:T(4,128)S(1)} %broadcast_multiply_fusion) | copy-start | bytes 6148
  239.0 14.8 %copy-start.28 = (f32[4,128]{1,0:T(4,128)}, f32[4,128]{1,0:T(4,128)S(1)}, u32[]{:S(2)}) copy-start(f32[4,128]{1,0:T(4,128)S(1)} %fusion.51) | copy-start | bytes 6148
  239.0 5.0 copy-start.11
  239.0 5.0 slice-start.3
  239.1 11.2 %slice-start = ((s8[4718592]{0:T(1024)(128)(4,1)}), s8[4194304]{0:T(1024)(128)(4,1)S(1)}, s32[]{:S(2)}) async-start(s8[4718592]{0:T(1024)(128)(4,1)} %bitcast.144), calls=%async_computation.30 | async-start | bytes 8388608
  244.0 6.2 copy-start.37
  244.1 6.2 slice-start.1
  250.3 3.5 copy-start.38
  253.8 3.0 copy-start.12
  254.5 1.2 copy-start.4
  254.5 1.4 copy-start.22
  255.9 0.9 copy-start.10
  258.5 160.5 %reduce-scatter.26.cloned.1.call-start = ((), (), s32[]{:S(2)}) async-start(), calls=%async_computation.18 | async-start | bytes 3932160 | tf_op jit(solution)/shard_map/reduce_scatter | solution.py:163
  328.7 21.8 %copy-start.5 = (bf16[4,256,768]{1,2,0:T(8,128)(2,1)S(1)}, bf16[4,256,768]{1,2,0:T(8,128)(2,1)}, u32[]{:S(2)}) copy-start(bf16[4,256,768]{1,2,0:T(8,128)(2,1)} %copy.64) | copy-start | bytes 4718596
  350.6 5.5 copy-start.1
  360.7 67.5 %reduce-scatter.28.cloned.1.call-start = ((), (), s32[]{:S(2)}) async-start(), calls=%async_computation.19 | async-start | bytes 2359296 | tf_op jit(solution)/shard_map/reduce_scatter | solution.py:170
  374.1 82.6 %reduce-scatter.30.cloned.1.call-start = ((), (), s32[]{:S(2)}) async-start(), calls=%async_computation.20 | async-start | bytes 2359296 | tf_op jit(solution)/shard_map/reduce_scatter | solution.py:176
  398.8 89.5 %reduce-scatter.34.cloned.1.call-start = ((), (), s32[]{:S(2)}) async-start(), calls=%async_computation.22 | async-start | bytes 1474560 | tf_op jit(solution)/shard_map/reduce_scatter | solution.py:193
  402.4 172.0 %reduce-scatter.38.cloned.1.call-start = ((), (), s32[]{:S(2)}) async-start(), calls=%async_computation.24 | async-start | bytes 5898240 | tf_op jit(solution)/shard_map/reduce_scatter | solution.py:199
  410.9 0.7 copy-start.19
  410.9 0.7 copy-start.29
  410.9 0.7 copy-start.31
  410.9 0.7 copy-start.35
  410.9 251.6 %reduce-scatter.36.cloned.1.call-start = ((), (), s32[]{:S(2)}) async-start(), calls=%async_computation.23 | async-start | bytes 5898240 | tf_op jit(solution)/shard_map/reduce_scatter | solution.py:196
  419.0 39.8 %copy-start.14 = (f32[4,128]{1,0:T(4,128)S(1)}, f32[4,128]{1,0:T(4,128)}, u32[]{:S(2)}) copy-start(f32[4,128]{1,0:T(4,128)} %copy-done.13) | copy-start | bytes 6148
  419.0 39.8 %copy-start.16 = (f32[4,128]{1,0:T(4,128)S(1)}, f32[4,128]{1,0:T(4,128)}, u32[]{:S(2)}) copy-start(f32[4,128]{1,0:T(4,128)} %copy-done.15) | copy-start | bytes 6148
  419.0 39.8 %copy-start.24 = (f32[768]{0:T(1024)S(1)}, f32[768]{0:T(1024)}, u32[]{:S(2)}) copy-start(f32[768]{0:T(1024)} %param.15) | copy-start | bytes 9220
  419.0 39.8 %copy-start.36 = (f32[768]{0:T(1024)S(1)}, f32[768]{0:T(1024)}, u32[]{:S(2)}) copy-start(f32[768]{0:T(1024)} %param.16) | copy-start | bytes 9220
  419.0 312.7 %reduce-scatter.32.cloned.1.call-start = ((), (), s32[]{:S(2)}) async-start(), calls=%async_computation.21 | async-start | bytes 4423680 | tf_op jit(solution)/shard_map/reduce_scatter | solution.py:190
  464.7 1.3 copy-start.33
  464.8 304.7 %reduce-scatter.42.cloned.1.call-start = ((), (), s32[]{:S(2)}) async-start(), calls=%async_computation.26 | async-start | bytes 442368
  490.2 4.1 copy-start.21
  490.2 316.4 %reduce-scatter.48.cloned.1.call-start = ((), (), s32[]{:S(2)}) async-start(), calls=%async_computation.29 | async-start | bytes 221184
  490.3 4.1 copy-start.2
  490.3 4.1 copy-start.25
  490.3 5.5 copy-start.26
  490.3 5.5 copy-start.27
  494.3 1.5 copy-start.6
  496.7 349.6 %reduce-scatter.46.cloned.1.call-start = ((), (), s32[]{:S(2)}) async-start(), calls=%async_computation.28 | async-start | bytes 1327104
  576.8 311.2 %reduce-scatter.44.cloned.1.call-start = ((), (), s32[]{:S(2)}) async-start(), calls=%async_computation.27 | async-start | bytes 1769472
  665.1 262.7 %reduce-scatter.40.cloned.1.call-start = ((), (), s32[]{:S(2)}) async-start(), calls=%async_computation.25 | async-start | bytes 1327104
  734.1 39.0 %copy-start.17 = (f32[4,128]{1,0:T(4,128)S(1)}, f32[4,128]{1,0:T(4,128)}, u32[]{:S(2)}) copy-start(f32[4,128]{1,0:T(4,128)} %copy-done.15) | copy-start | bytes 6148
  734.1 39.0 %copy-start.23 = (f32[4,128]{1,0:T(4,128)S(1)}, f32[4,128]{1,0:T(4,128)}, u32[]{:S(2)}) copy-start(f32[4,128]{1,0:T(4,128)} %copy-done.22) | copy-start | bytes 6148
Sparse Core Ops, SparseCore 0:
  15.8 29.8 all-gather.11
  47.2 27.1 all-gather.7
  76.6 28.5 all-gather.9
  177.7 57.8 reduce-scatter.23
  258.7 28.5 all-gather.13
  360.9 38.8 reduce-scatter.25
  402.0 26.1 reduce-scatter.27
  430.4 26.1 reduce-scatter.29
  458.9 29.3 reduce-scatter.33
  490.4 83.8 reduce-scatter.37
  576.7 85.7 reduce-scatter.35
  664.7 67.0 reduce-scatter.31
  735.4 34.0 reduce-scatter.41
  772.9 33.6 reduce-scatter.47
  809.7 36.6 reduce-scatter.45
  849.5 38.3 reduce-scatter.43
  891.0 36.6 reduce-scatter.39
